TPU v7x, 32 devices: a whole 2x2x4 slice. The times are simulated.
32 devices in a mesh: groups: 2 (over y), seq: 4 (over z), head: 4 (over x, core).
Axes of the slice: x: 2, y: 2, z: 4, core: 2. Of those that a mesh axis runs over, the one named last changes fastest.
Arguments:
- cand_feats: bfloat16 [32768, 512], P(('groups', 'seq'), 'head'), parts along dimension 0, may hold values from -6 to 6
- w_query: bfloat16 [512, 512], P(None, 'head'), may hold values from -0.25 to 0.25
- w_gate: bfloat16 [512, 512], replicated, may hold values from -0.25 to 0.25
- w_out: bfloat16 [512, 512], replicated, may hold values from -0.25 to 0.25
- w_up: bfloat16 [512, 1024], replicated, may hold values from -0.25 to 0.25
- w_down: bfloat16 [1024, 512], replicated, may hold values from -0.1875 to 0.1875
- norm_gain: float32 [512], replicated, may hold values from 0.5 to 1.5
- cache_keys: bfloat16 [32, 16384, 512], P('groups', 'seq', 'head'), parts along dimension 0, may hold values from -6 to 6
- cache_values: bfloat16 [32, 16384, 512], P('groups', 'seq', 'head'), parts along dimension 0, may hold values from -6 to 6
- history_items: int32 [32, 16384], P('groups', 'seq'), parts along dimension 0, may hold values from 0 to 63
- buckets: int32 [32, 16384], P('groups', 'seq'), parts along dimension 0, may hold values from 0 to 127
- lengths: int32 [32], P('groups'), parts along dimension 0, may hold values from 1 to 16384
- cand_ids: int32 [32, 1024], P('groups'), parts along dimension 0, may hold values from 0 to 63
- bucket_bias: float32 [128, 8], P(None, 'head'), may hold values from -4 to 4
- repeat_bias: float32 [8], P('head'), may hold values from 0.5 to 3
Outputs:
- scored: bfloat16 [32768, 512], P(('groups', 'seq', 'head')), parts along dimension 0
There are 2 independent parts, one for each index of `groups`. A program takes and returns all parts, laid end to end along the dimension named above; an argument that names none is the same for every part. Nothing has to cross between parts.
Inputs may be any that keep to these rules, and one draw needn't show every extreme that they name: `lengths`: history positions at or past a user's length are ignored.
All inputs are finite; a program needn't handle non-finite values.
Results may differ from a plain program's by a relative error of at most 0.014.
Values may be sent and summed in bfloat16 or wider, within the bound.
A program may use at most 192 MiB of HBM per device.

v0:
```python
import math

import jax
import jax.numpy as jnp
from jax import lax
from jax.sharding import PartitionSpec as P

DH = 64


def silu_value(value):
    return value / (1.0 + jnp.exp(-value))


def block_sum(
    query_user,
    key_slab,
    value_slab,
    item_slab,
    bucket_slab,
    first_pos,
    user_length,
    cand_row,
    bias_table,
    repeat_gain,
    shard_span,
):
    block_size = key_slab.shape[0]
    local_heads = query_user.shape[1]
    group_count = block_size // shard_span
    scores = jnp.einsum("chd,khd->chk", query_user, key_slab, preferred_element_type=jnp.float32)
    onehot_table = (
        bucket_slab[:, None] == jnp.arange(bias_table.shape[0], dtype=jnp.int32)[None, :]
    ).astype(jnp.float32)
    offset = jnp.dot(onehot_table, bias_table, precision=lax.Precision.HIGHEST)
    repeat_hits = (cand_row[:, None] == item_slab[None, :]).astype(jnp.float32)
    scale = 1.0 / math.sqrt(query_user.shape[2])
    scores = (
        scores * scale + offset.T[None, :, :] + repeat_gain[None, :, None] * repeat_hits[:, None, :]
    )
    positions = first_pos + jnp.arange(block_size, dtype=jnp.int32)
    live_mask = (positions < user_length).astype(jnp.float32)
    weights = (silu_value(scores) * live_mask[None, None, :]).astype(jnp.bfloat16)
    weights = weights.reshape(query_user.shape[0], local_heads, group_count, shard_span)
    grouped = value_slab.reshape(group_count, shard_span, local_heads, value_slab.shape[2])
    block_parts = jnp.einsum(
        "chgk,gkhd->gchd", weights, grouped, preferred_element_type=jnp.float32
    )
    rounded = lax.optimization_barrier(block_parts.astype(jnp.bfloat16))
    return jnp.sum(rounded.astype(jnp.float32), axis=0)


def attend_user(
    query_user,
    key_user,
    value_user,
    item_user,
    bucket_user,
    first_pos,
    user_length,
    cand_row,
    bias_table,
    repeat_gain,
    shard_span,
):
    total_len = key_user.shape[0]
    group_count = math.gcd(total_len // shard_span, max(1, 512 // shard_span))
    block_size = shard_span * group_count
    turn_count = total_len // block_size
    zero_sum = jnp.zeros(query_user.shape, jnp.float32)

    def accumulate(turn_index, running):
        offset_pos = turn_index * block_size
        slab_first = first_pos + offset_pos
        added = block_sum(
            query_user,
            key_user,
            value_user,
            item_user,
            bucket_user,
            slab_first,
            user_length,
            cand_row,
            bias_table,
            repeat_gain,
            shard_span,
        )
        return running + added

    return lax.fori_loop(0, turn_count, accumulate, zero_sum)


def run_users(
    grouped_q,
    key_rows,
    value_rows,
    item_rows,
    bucket_rows,
    first_pos,
    user_lengths,
    cand_rows,
    bias_table,
    repeat_gain,
    shard_span,
):
    user_count = grouped_q.shape[0]
    local_heads = grouped_q.shape[2]
    head_size = grouped_q.shape[3]
    keyed = key_rows.reshape(user_count, key_rows.shape[1], local_heads, head_size)
    valued = value_rows.reshape(user_count, value_rows.shape[1], local_heads, head_size)

    def one_user(inputs):
        query_user, key_user, value_user, item_user, bucket_user, user_length, cand_row = inputs
        return attend_user(
            query_user,
            key_user,
            value_user,
            item_user,
            bucket_user,
            first_pos,
            user_length,
            cand_row,
            bias_table,
            repeat_gain,
            shard_span,
        )

    return lax.map(
        one_user, (grouped_q, keyed, valued, item_rows, bucket_rows, user_lengths, cand_rows)
    )


def local(
    cand_feats,
    w_query,
    w_gate,
    w_out,
    w_up,
    w_down,
    norm_gain,
    cache_keys,
    cache_values,
    history_items,
    buckets,
    lengths,
    cand_ids,
    bucket_bias,
    repeat_bias,
):
    features = lax.all_gather(cand_feats, "head", axis=1, tiled=True)
    queries_own = jnp.dot(features, w_query, preferred_element_type=jnp.float32).astype(
        jnp.bfloat16
    )
    user_count = lengths.shape[0]
    per_user = cand_ids.shape[1]
    shard_span = cache_keys.shape[1]
    local_width = cache_keys.shape[2]
    local_heads = local_width // DH
    seq_pos = lax.axis_index("seq")
    gathered = lax.all_gather(queries_own, "seq", axis=0, tiled=True)
    grouped_q = gathered.reshape(user_count, per_user, local_heads, DH)
    result = run_users(
        grouped_q,
        cache_keys,
        cache_values,
        history_items,
        buckets,
        seq_pos * shard_span,
        lengths,
        cand_ids,
        bucket_bias,
        repeat_bias,
        shard_span,
    )
    partial_rows = result.reshape(user_count * per_user, local_width)
    own_sum = lax.psum_scatter(
        partial_rows.astype(jnp.bfloat16), "seq", scatter_dimension=0, tiled=True
    ).astype(jnp.float32)
    pieces = lax.all_to_all(
        own_sum.astype(jnp.bfloat16), "head", split_axis=0, concat_axis=1, tiled=True
    ).astype(own_sum.dtype)
    row_count = pieces.shape[0]
    own_rows = lax.dynamic_slice_in_dim(features, lax.axis_index("head") * row_count, row_count, 0)
    center = pieces - jnp.mean(pieces, axis=1, keepdims=True)
    normed = (
        center
        * lax.rsqrt(jnp.mean(center * center, axis=1, keepdims=True) + 1e-05)
        * norm_gain[None, :]
    )
    gate_value = silu_value(jnp.dot(own_rows, w_gate, preferred_element_type=jnp.float32))
    mixed = (normed * gate_value).astype(jnp.bfloat16)
    state_sum = own_rows.astype(jnp.float32) + jnp.dot(
        mixed, w_out, preferred_element_type=jnp.float32
    )
    hidden = silu_value(
        jnp.dot(state_sum.astype(jnp.bfloat16), w_up, preferred_element_type=jnp.float32)
    ).astype(jnp.bfloat16)
    return (state_sum + jnp.dot(hidden, w_down, preferred_element_type=jnp.float32)).astype(
        jnp.bfloat16
    )


def solution(mesh):
    in_specs = (
        P(("groups", "seq"), "head"),
        P(None, "head"),
        P(),
        P(),
        P(),
        P(),
        P(),
        P("groups", "seq", "head"),
        P("groups", "seq", "head"),
        P("groups", "seq"),
        P("groups", "seq"),
        P("groups"),
        P("groups", None),
        P(None, "head"),
        P("head"),
    )
    out_specs = P(("groups", "seq", "head"), None)
    return jax.shard_map(local, mesh=mesh, in_specs=in_specs, out_specs=out_specs, check_vma=False)
```

profile of v0, /device:TPU:0, one launch (start us, length us, event | category | flops | bytes accessed | tf_op | source)
XLA Modules:
  0.0 763.6 jit_solution(261983863570828236)
XLA Ops:
  7.3 39.3 %all-gather.3.cloned.1.call-done = bf16[4096,512]{1,0:T(8,128)(2,1)} async-done(((bf16[4096,128]{1,0:T(8,128)(2,1)}), bf16[4096,512]{1,0:T(8,128)(2,1)}) %all-gather.3.cloned.1.call-update) | async-done | bytes 4194320 | tf_op jit(solution)/shard_map/all_gather | solution.py:150
  51.1 21.2 %copy.21 = bf16[16,4096,128]{1,2,0:T(8,128)(2,1)} copy(bf16[16,4096,128]{2,1,0:T(8,128)(2,1)} %param.25) | data formatting | bytes 33554432 | tf_op args[8]
  72.4 20.9 %copy.22 = bf16[16,4096,128]{1,2,0:T(8,128)(2,1)} copy(bf16[16,4096,128]{2,1,0:T(8,128)(2,1)} %param.24) | data formatting | bytes 33554432 | tf_op args[7]
  93.3 38.7 %all-gather.5.cloned.1.call-done = bf16[16384,128]{1,0:T(8,128)(2,1)} async-done(((bf16[4096,128]{1,0:T(8,128)(2,1)}), bf16[16384,128]{1,0:T(8,128)(2,1)}) %all-gather.5.cloned.1.call-update) | async-done | bytes 4194320 | tf_op jit(solution)/shard_map/all_gather | solution.py:160
  132.0 14.7 %reshape.92 = bf16[16,1024,2,64]{3,2,1,0:T(2,128)(2,1)} reshape(bf16[16384,128]{1,0:T(8,128)(2,1)} %all-gather.5.cloned.1.call-done) | data formatting | bytes 8388608 | tf_op jit(solution)/shard_map/reshape | solution.py:161
  146.7 20.2 %copy.24 = bf16[16,1024,2,64]{1,3,2,0:T(8,128)(2,1)} copy(bf16[16,1024,2,64]{3,2,1,0:T(2,128)(2,1)} %reshape.92) | data formatting | bytes 8388608 | tf_op jit(solution)/shard_map/while | solution.py:128
  166.9 474.1 %while.11 = (s32[]{:T(128)}, bf16[16,1024,2,64]{1,3,2,0:T(8,128)(2,1)}, bf16[16,4096,2,64]{1,3,2,0:T(8,128)(2,1)}, bf16[16,4096,2,64]{1,3,2,0:T(8,128)(2,1)}, bf...) while((s32[]{:T(128)}, ...), condition=%wide.region_1.2_spmd, body=%wide.region_0.1_spmd.sunk | while | flops 2244751360 | bytes 37174432 | solution.py:128
  177.4 18.4 %fusion.64 = bf16[1,1024,2,64]{1,3,2,0:T(8,128)(2,1)S(1)} fusion(f32[4096]{0:T(1024)S(1)} %fusion.63, f32[1024,4096]{0,1:T(8,128)} %compare_convert_fusion.2, f32[2]{0:T(128)S(1)} %get-tuple-element.267, f32[2,4096]{1,0:T(2,128)S(1)} %convolution_bitcast_fusion.2, bf16[16,4096,2,64]{1,3,2,0:T(8,128)(2,1)} %get-tuple-element.263, ...), kind=kOutput, calls=%fused_computation.8.clone.1 | convolution fusion | flops 2223112192 | bytes 19449352 | tf_op jit(solution)/shard_map/while/body/eval_jaxpr/while/body/eval_jaxpr/chgk,gkhd->gchd/dot_general | solution.py:46
  207.0 18.4 %fusion.64 = bf16[1,1024,2,64]{1,3,2,0:T(8,128)(2,1)S(1)} fusion(f32[4096]{0:T(1024)S(1)} %fusion.63, f32[1024,4096]{0,1:T(8,128)} %compare_convert_fusion.2, f32[2]{0:T(128)S(1)} %get-tuple-element.267, f32[2,4096]{1,0:T(2,128)S(1)} %convolution_bitcast_fusion.2, bf16[16,4096,2,64]{1,3,2,0:T(8,128)(2,1)} %get-tuple-element.263, ...), kind=kOutput, calls=%fused_computation.8.clone.1 | convolution fusion | flops 2223112192 | bytes 19449352 | tf_op jit(solution)/shard_map/while/body/eval_jaxpr/while/body/eval_jaxpr/chgk,gkhd->gchd/dot_general | solution.py:46
  236.7 18.4 %fusion.64 = bf16[1,1024,2,64]{1,3,2,0:T(8,128)(2,1)S(1)} fusion(f32[4096]{0:T(1024)S(1)} %fusion.63, f32[1024,4096]{0,1:T(8,128)} %compare_convert_fusion.2, f32[2]{0:T(128)S(1)} %get-tuple-element.267, f32[2,4096]{1,0:T(2,128)S(1)} %convolution_bitcast_fusion.2, bf16[16,4096,2,64]{1,3,2,0:T(8,128)(2,1)} %get-tuple-element.263, ...), kind=kOutput, calls=%fused_computation.8.clone.1 | convolution fusion | flops 2223112192 | bytes 19449352 | tf_op jit(solution)/shard_map/while/body/eval_jaxpr/while/body/eval_jaxpr/chgk,gkhd->gchd/dot_general | solution.py:46
  266.3 18.4 %fusion.64 = bf16[1,1024,2,64]{1,3,2,0:T(8,128)(2,1)S(1)} fusion(f32[4096]{0:T(1024)S(1)} %fusion.63, f32[1024,4096]{0,1:T(8,128)} %compare_convert_fusion.2, f32[2]{0:T(128)S(1)} %get-tuple-element.267, f32[2,4096]{1,0:T(2,128)S(1)} %convolution_bitcast_fusion.2, bf16[16,4096,2,64]{1,3,2,0:T(8,128)(2,1)} %get-tuple-element.263, ...), kind=kOutput, calls=%fused_computation.8.clone.1 | convolution fusion | flops 2223112192 | bytes 19449352 | tf_op jit(solution)/shard_map/while/body/eval_jaxpr/while/body/eval_jaxpr/chgk,gkhd->gchd/dot_general | solution.py:46
  295.9 18.4 %fusion.64 = bf16[1,1024,2,64]{1,3,2,0:T(8,128)(2,1)S(1)} fusion(f32[4096]{0:T(1024)S(1)} %fusion.63, f32[1024,4096]{0,1:T(8,128)} %compare_convert_fusion.2, f32[2]{0:T(128)S(1)} %get-tuple-element.267, f32[2,4096]{1,0:T(2,128)S(1)} %convolution_bitcast_fusion.2, bf16[16,4096,2,64]{1,3,2,0:T(8,128)(2,1)} %get-tuple-element.263, ...), kind=kOutput, calls=%fused_computation.8.clone.1 | convolution fusion | flops 2223112192 | bytes 19449352 | tf_op jit(solution)/shard_map/while/body/eval_jaxpr/while/body/eval_jaxpr/chgk,gkhd->gchd/dot_general | solution.py:46
  325.5 18.4 %fusion.64 = bf16[1,1024,2,64]{1,3,2,0:T(8,128)(2,1)S(1)} fusion(f32[4096]{0:T(1024)S(1)} %fusion.63, f32[1024,4096]{0,1:T(8,128)} %compare_convert_fusion.2, f32[2]{0:T(128)S(1)} %get-tuple-element.267, f32[2,4096]{1,0:T(2,128)S(1)} %convolution_bitcast_fusion.2, bf16[16,4096,2,64]{1,3,2,0:T(8,128)(2,1)} %get-tuple-element.263, ...), kind=kOutput, calls=%fused_computation.8.clone.1 | convolution fusion | flops 2223112192 | bytes 19449352 | tf_op jit(solution)/shard_map/while/body/eval_jaxpr/while/body/eval_jaxpr/chgk,gkhd->gchd/dot_general | solution.py:46
  355.2 18.4 %fusion.64 = bf16[1,1024,2,64]{1,3,2,0:T(8,128)(2,1)S(1)} fusion(f32[4096]{0:T(1024)S(1)} %fusion.63, f32[1024,4096]{0,1:T(8,128)} %compare_convert_fusion.2, f32[2]{0:T(128)S(1)} %get-tuple-element.267, f32[2,4096]{1,0:T(2,128)S(1)} %convolution_bitcast_fusion.2, bf16[16,4096,2,64]{1,3,2,0:T(8,128)(2,1)} %get-tuple-element.263, ...), kind=kOutput, calls=%fused_computation.8.clone.1 | convolution fusion | flops 2223112192 | bytes 19449352 | tf_op jit(solution)/shard_map/while/body/eval_jaxpr/while/body/eval_jaxpr/chgk,gkhd->gchd/dot_general | solution.py:46
  384.8 18.4 %fusion.64 = bf16[1,1024,2,64]{1,3,2,0:T(8,128)(2,1)S(1)} fusion(f32[4096]{0:T(1024)S(1)} %fusion.63, f32[1024,4096]{0,1:T(8,128)} %compare_convert_fusion.2, f32[2]{0:T(128)S(1)} %get-tuple-element.267, f32[2,4096]{1,0:T(2,128)S(1)} %convolution_bitcast_fusion.2, bf16[16,4096,2,64]{1,3,2,0:T(8,128)(2,1)} %get-tuple-element.263, ...), kind=kOutput, calls=%fused_computation.8.clone.1 | convolution fusion | flops 2223112192 | bytes 19449352 | tf_op jit(solution)/shard_map/while/body/eval_jaxpr/while/body/eval_jaxpr/chgk,gkhd->gchd/dot_general | solution.py:46
  414.4 18.4 %fusion.64 = bf16[1,1024,2,64]{1,3,2,0:T(8,128)(2,1)S(1)} fusion(f32[4096]{0:T(1024)S(1)} %fusion.63, f32[1024,4096]{0,1:T(8,128)} %compare_convert_fusion.2, f32[2]{0:T(128)S(1)} %get-tuple-element.267, f32[2,4096]{1,0:T(2,128)S(1)} %convolution_bitcast_fusion.2, bf16[16,4096,2,64]{1,3,2,0:T(8,128)(2,1)} %get-tuple-element.263, ...), kind=kOutput, calls=%fused_computation.8.clone.1 | convolution fusion | flops 2223112192 | bytes 19449352 | tf_op jit(solution)/shard_map/while/body/eval_jaxpr/while/body/eval_jaxpr/chgk,gkhd->gchd/dot_general | solution.py:46
  444.1 18.4 %fusion.64 = bf16[1,1024,2,64]{1,3,2,0:T(8,128)(2,1)S(1)} fusion(f32[4096]{0:T(1024)S(1)} %fusion.63, f32[1024,4096]{0,1:T(8,128)} %compare_convert_fusion.2, f32[2]{0:T(128)S(1)} %get-tuple-element.267, f32[2,4096]{1,0:T(2,128)S(1)} %convolution_bitcast_fusion.2, bf16[16,4096,2,64]{1,3,2,0:T(8,128)(2,1)} %get-tuple-element.263, ...), kind=kOutput, calls=%fused_computation.8.clone.1 | convolution fusion | flops 2223112192 | bytes 19449352 | tf_op jit(solution)/shard_map/while/body/eval_jaxpr/while/body/eval_jaxpr/chgk,gkhd->gchd/dot_general | solution.py:46
  473.7 18.4 %fusion.64 = bf16[1,1024,2,64]{1,3,2,0:T(8,128)(2,1)S(1)} fusion(f32[4096]{0:T(1024)S(1)} %fusion.63, f32[1024,4096]{0,1:T(8,128)} %compare_convert_fusion.2, f32[2]{0:T(128)S(1)} %get-tuple-element.267, f32[2,4096]{1,0:T(2,128)S(1)} %convolution_bitcast_fusion.2, bf16[16,4096,2,64]{1,3,2,0:T(8,128)(2,1)} %get-tuple-element.263, ...), kind=kOutput, calls=%fused_computation.8.clone.1 | convolution fusion | flops 2223112192 | bytes 19449352 | tf_op jit(solution)/shard_map/while/body/eval_jaxpr/while/body/eval_jaxpr/chgk,gkhd->gchd/dot_general | solution.py:46
  503.3 18.4 %fusion.64 = bf16[1,1024,2,64]{1,3,2,0:T(8,128)(2,1)S(1)} fusion(f32[4096]{0:T(1024)S(1)} %fusion.63, f32[1024,4096]{0,1:T(8,128)} %compare_convert_fusion.2, f32[2]{0:T(128)S(1)} %get-tuple-element.267, f32[2,4096]{1,0:T(2,128)S(1)} %convolution_bitcast_fusion.2, bf16[16,4096,2,64]{1,3,2,0:T(8,128)(2,1)} %get-tuple-element.263, ...), kind=kOutput, calls=%fused_computation.8.clone.1 | convolution fusion | flops 2223112192 | bytes 19449352 | tf_op jit(solution)/shard_map/while/body/eval_jaxpr/while/body/eval_jaxpr/chgk,gkhd->gchd/dot_general | solution.py:46
  532.9 18.4 %fusion.64 = bf16[1,1024,2,64]{1,3,2,0:T(8,128)(2,1)S(1)} fusion(f32[4096]{0:T(1024)S(1)} %fusion.63, f32[1024,4096]{0,1:T(8,128)} %compare_convert_fusion.2, f32[2]{0:T(128)S(1)} %get-tuple-element.267, f32[2,4096]{1,0:T(2,128)S(1)} %convolution_bitcast_fusion.2, bf16[16,4096,2,64]{1,3,2,0:T(8,128)(2,1)} %get-tuple-element.263, ...), kind=kOutput, calls=%fused_computation.8.clone.1 | convolution fusion | flops 2223112192 | bytes 19449352 | tf_op jit(solution)/shard_map/while/body/eval_jaxpr/while/body/eval_jaxpr/chgk,gkhd->gchd/dot_general | solution.py:46
  562.6 18.4 %fusion.64 = bf16[1,1024,2,64]{1,3,2,0:T(8,128)(2,1)S(1)} fusion(f32[4096]{0:T(1024)S(1)} %fusion.63, f32[1024,4096]{0,1:T(8,128)} %compare_convert_fusion.2, f32[2]{0:T(128)S(1)} %get-tuple-element.267, f32[2,4096]{1,0:T(2,128)S(1)} %convolution_bitcast_fusion.2, bf16[16,4096,2,64]{1,3,2,0:T(8,128)(2,1)} %get-tuple-element.263, ...), kind=kOutput, calls=%fused_computation.8.clone.1 | convolution fusion | flops 2223112192 | bytes 19449352 | tf_op jit(solution)/shard_map/while/body/eval_jaxpr/while/body/eval_jaxpr/chgk,gkhd->gchd/dot_general | solution.py:46
  592.2 18.4 %fusion.64 = bf16[1,1024,2,64]{1,3,2,0:T(8,128)(2,1)S(1)} fusion(f32[4096]{0:T(1024)S(1)} %fusion.63, f32[1024,4096]{0,1:T(8,128)} %compare_convert_fusion.2, f32[2]{0:T(128)S(1)} %get-tuple-element.267, f32[2,4096]{1,0:T(2,128)S(1)} %convolution_bitcast_fusion.2, bf16[16,4096,2,64]{1,3,2,0:T(8,128)(2,1)} %get-tuple-element.263, ...), kind=kOutput, calls=%fused_computation.8.clone.1 | convolution fusion | flops 2223112192 | bytes 19449352 | tf_op jit(solution)/shard_map/while/body/eval_jaxpr/while/body/eval_jaxpr/chgk,gkhd->gchd/dot_general | solution.py:46
  621.8 18.4 %fusion.64 = bf16[1,1024,2,64]{1,3,2,0:T(8,128)(2,1)S(1)} fusion(f32[4096]{0:T(1024)S(1)} %fusion.63, f32[1024,4096]{0,1:T(8,128)} %compare_convert_fusion.2, f32[2]{0:T(128)S(1)} %get-tuple-element.267, f32[2,4096]{1,0:T(2,128)S(1)} %convolution_bitcast_fusion.2, bf16[16,4096,2,64]{1,3,2,0:T(8,128)(2,1)} %get-tuple-element.263, ...), kind=kOutput, calls=%fused_computation.8.clone.1 | convolution fusion | flops 2223112192 | bytes 19449352 | tf_op jit(solution)/shard_map/while/body/eval_jaxpr/while/body/eval_jaxpr/chgk,gkhd->gchd/dot_general | solution.py:46
  650.2 75.4 %reduce-scatter.2.cloned.1.call-done = bf16[4096,128]{0,1:T(8,128)(2,1)} async-done(((bf16[16384,128]{0,1:T(8,128)(2,1)}), bf16[4096,128]{0,1:T(8,128)(2,1)}) %reduce-scatter.2.cloned.1.call-update) | async-done | bytes 1048592 | tf_op jit(solution)/shard_map/reduce_scatter | solution.py:176
  (143 shorter events, 225.7 us)
Async XLA Ops:
  6.5 744.9 %copy-start = (bf16[1024,512]{1,0:T(8,128)(2,1)S(1)}, bf16[1024,512]{1,0:T(8,128)(2,1)}, u32[]{:S(2)}) copy-start(bf16[1024,512]{1,0:T(8,128)(2,1)} %param.22) | copy-start | bytes 3145732
  6.5 40.1 %all-gather.3.cloned.1.call-start = ((), (), s32[]{:S(2)}) async-start(), calls=%async_computation.2 | async-start | bytes 5242880 | tf_op jit(solution)/shard_map/all_gather | solution.py:150
  7.3 124.7 %all-gather.5.cloned.1.call-start = ((), (), s32[]{:S(2)}) async-start(), calls=%async_computation.3 | async-start | bytes 5242880 | tf_op jit(solution)/shard_map/all_gather | solution.py:160
  51.1 674.5 %reduce-scatter.2.cloned.1.call-start = ((), (), s32[]{:S(2)}) async-start(), calls=%async_computation.4 | async-start | bytes 5242880 | tf_op jit(solution)/shard_map/reduce_scatter | solution.py:176
  146.7 20.2 %copy-start.3 = (f32[128,2]{0,1:T(2,128)S(1)}, f32[128,2]{0,1:T(2,128)}, u32[]{:S(2)}) copy-start(f32[128,2]{0,1:T(2,128)} %param.30) | copy-start | bytes 3076
  146.7 20.2 %copy-start.4 = (f32[2]{0:T(128)S(1)}, f32[2]{0:T(128)}, u32[]{:S(2)}) copy-start(f32[2]{0:T(128)} %param.31) | copy-start | bytes 28
  146.7 20.2 %copy-start.5 = (s32[16]{0:T(128)S(1)}, s32[16]{0:T(128)}, u32[]{:S(2)}) copy-start(s32[16]{0:T(128)} %param.28) | copy-start | bytes 196
  650.2 96.4 %copy-start.2 = (f32[512]{0:T(512)S(1)}, f32[512]{0:T(512)}, u32[]{:S(2)}) copy-start(f32[512]{0:T(512)} %param.23) | copy-start | bytes 6148
  727.9 17.9 %all-to-all-start = ((bf16[4,1024,128]{2,1,0:T(8,128)(2,1)}), bf16[4,1024,128]{2,1,0:T(8,128)(2,1)S(1)}, u32[]{:S(2)}, u32[]{:S(2)}) async-start(bf16[4,1024,128]{2,1,0:T(8,128)(2,1)} %bitcast.13), calls=%async_computation.1 | async-start | bytes 2097152 | tf_op jit(solution)/shard_map/all_to_all | solution.py:179
  746.5 4.9 copy-start.1
Sparse Core Ops, SparseCore 0:
  8.9 37.7 all-gather.2
  51.2 80.7 all-gather.4
  650.3 75.2 reduce-scatter.1
where the time goes:
time: 767 us; the launch traced here: 764 us
  matrix products  332 us (43%)
  waiting for transfers between devices  169 us (22%)
  local copies, waits for them, and re-layouts  126 us (16%)
  other arithmetic  120 us (16%)
  between operations  13.2 us (2%)
    dot_general x16, matrix products, block_sum(): jnp.einsum('chgk,gkhd->gchd', weights, grouped, preferred_element_type=jn...  294 us
    convert_element_type x16, other arithmetic, block_sum(): repeat_hits = (cand_row[:, None] == item_slab[None, :]).astype(jnp.float32)  96.9 us
    reduce_scatter x1, waiting for transfers between devices, local(): lax.psum_scatter(partial_rows.astype(jnp.bfloat16), 'seq', scatter_dimens...  75.4 us
    unnamed x15, local copies, waits for them, and re-layouts  46.8 us
    all_gather x1, waiting for transfers between devices, local(): features = lax.all_gather(cand_feats, 'head', axis=1, tiled=True)  39.3 us
    all_gather x1, waiting for transfers between devices, local(): gathered = lax.all_gather(queries_own, 'seq', axis=0, tiled=True)  38.7 us
    dynamic_slice x48, local copies, waits for them, and re-layouts, run_users(): lax.map(one_user, (grouped_q, keyed, valued, item_rows, bucket_rows, user...  37.8 us
    dot_general x16, matrix products, block_sum(): offset = jnp.dot(onehot_table, bias_table, precision=lax.Precision.HIGHEST)  23.1 us
  transfers between devices with their start and end apart: 4, of which 4 were waited for; matrix products, arithmetic and copies ran while one was open for 6% of the time, Pallas kernels for 0%

commit v1 on v0

v1 whole, which is shorter than its diff:
```python
import functools
import math

import jax
import jax.numpy as jnp
from jax import lax
from jax.experimental import pallas as pl
from jax.experimental.pallas import tpu as pltpu
from jax.sharding import PartitionSpec as P

DH = 64
ITEMS = 64
LANES = 2 * DH
KEYS = 1024
ROWS = 1024


def silu_value(value):
    return value / (1.0 + jnp.exp(-value))


def attend_kernel(
    live_ref,
    gain_ref,
    q_ref,
    same_ref,
    tail_ref,
    key_ref,
    value_ref,
    item_ref,
    bucket_ref,
    table_ref,
    out_ref,
    q_first,
    q_second,
    total,
    *,
    keys,
    rows,
    first_user,
):
    pair = pl.program_id(0)
    user = pl.program_id(1)
    live = live_ref[first_user + user]
    low_lanes = lax.broadcasted_iota(jnp.int32, (1, LANES), 1) < DH
    low_row = low_lanes.astype(jnp.bfloat16)
    high_row = 1 - low_row
    queries = q_ref[...]
    same = same_ref[0]
    q_first[:, :LANES] = queries * low_row + same * high_row
    q_second[:, :LANES] = same * low_row + queries * high_row
    q_first[:, LANES:] = tail_ref[0]
    q_second[:, LANES:] = tail_ref[0]
    total[...] = jnp.zeros_like(total)
    table = table_ref[pair]

    def step(index, carry):
        start = pl.multiple_of(index * keys, keys)
        window = pl.ds(start, keys)
        keyed = key_ref[0, window, :].T
        items = item_ref[0, :, window]
        hits = lax.broadcasted_iota(jnp.int32, (ITEMS, keys), 0) == items
        bucket_hits = (
            lax.broadcasted_iota(jnp.int32, (table.shape[1], keys), 0) == bucket_ref[0, :, window]
        )
        bias = jnp.dot(
            table,
            bucket_hits.astype(jnp.float32).astype(jnp.bfloat16),
            preferred_element_type=jnp.float32,
        ).astype(jnp.bfloat16)

        def gains(which):
            return jnp.where(hits, gain_ref[pair, which], 0.0).astype(jnp.bfloat16)

        depth_first = jnp.concatenate([keyed[:DH], gains(0), gains(1), bias[:DH]], axis=0)
        depth_second = jnp.concatenate([gains(2), keyed[DH:], gains(3), bias[DH:]], axis=0)
        place = start + lax.broadcasted_iota(jnp.int32, (keys, LANES), 0)
        lane = lax.broadcasted_iota(jnp.int32, (keys, LANES), 1)
        values = value_ref[0, window, :].astype(jnp.float32)
        alive = place < live
        values_first = jnp.where(alive & (lane < DH), values, 0.0).astype(jnp.bfloat16)
        values_second = jnp.where(alive & (lane >= DH), values, 0.0).astype(jnp.bfloat16)
        for base in range(0, total.shape[0], rows):
            span = slice(base, base + rows)
            half = jnp.dot(q_first[span, :], depth_first, preferred_element_type=jnp.float32)
            act_first = (half + half * jnp.tanh(half)).astype(jnp.bfloat16)
            half = jnp.dot(q_second[span, :], depth_second, preferred_element_type=jnp.float32)
            act_second = (half + half * jnp.tanh(half)).astype(jnp.bfloat16)
            total[span, :] += jnp.dot(
                act_first, values_first, preferred_element_type=jnp.float32
            ) + jnp.dot(act_second, values_second, preferred_element_type=jnp.float32)
        return carry

    count = key_ref.shape[1] // keys
    used = jnp.clip((live + keys - 1) // keys, 0, count)
    lax.fori_loop(0, used, step, 0)
    out_ref[...] = total[...].astype(out_ref.dtype)


def attend(queries, packed, first_user, user_count):
    live, gains, same, tail, keys_all, values_all, items, buckets, table = packed
    per_user = same.shape[1]
    width = queries.shape[1]
    pairs = width // LANES
    span = keys_all.shape[1]
    keys = math.gcd(span, KEYS)
    rows = math.gcd(per_user, ROWS)
    of_user = lambda p, u, *_: (first_user + u, 0, 0)
    of_pair = lambda p, u, *_: (first_user + u, 0, p)
    scores = user_count * per_user * span * 2 * pairs
    return pl.pallas_call(
        functools.partial(attend_kernel, keys=keys, rows=rows, first_user=first_user),
        out_shape=jax.ShapeDtypeStruct(queries.shape, jnp.bfloat16),
        grid_spec=pltpu.PrefetchScalarGridSpec(
            num_scalar_prefetch=2,
            grid=(pairs, user_count),
            in_specs=[
                pl.BlockSpec((per_user, LANES), lambda p, u, *_: (u, p)),
                pl.BlockSpec((1, per_user, LANES), of_user),
                pl.BlockSpec((1, per_user, LANES), of_user),
                pl.BlockSpec((1, span, LANES), of_pair),
                pl.BlockSpec((1, span, LANES), of_pair),
                pl.BlockSpec((1, 1, span), of_user),
                pl.BlockSpec((1, 1, span), of_user),
                pl.BlockSpec(table.shape, lambda p, u, *_: (0, 0, 0)),
            ],
            out_specs=pl.BlockSpec((per_user, LANES), lambda p, u, *_: (u, p)),
            scratch_shapes=[
                pltpu.VMEM((per_user, 2 * LANES), jnp.bfloat16),
                pltpu.VMEM((per_user, 2 * LANES), jnp.bfloat16),
                pltpu.VMEM((per_user, LANES), jnp.float32),
            ],
        ),
        compiler_params=pltpu.CompilerParams(
            dimension_semantics=("arbitrary", "arbitrary"), vmem_limit_bytes=56 << 20
        ),
        cost_estimate=pl.CostEstimate(
            flops=scores * 512,
            bytes_accessed=4 * user_count * (span + per_user) * width,
            transcendentals=scores,
        ),
    )(live, gains, queries, same, tail, keys_all, values_all, items, buckets, table)


def split_parts(value, count):
    parts = []
    for _ in range(count):
        part = lax.reduce_precision(value, 8, 7)
        parts.append(part)
        value = value - part
    return parts


def pack_tables(keys_all, values_all, items, buckets, lengths, cand_ids, bias_table, gain, first_pos):
    width = keys_all.shape[2]
    pad = -width % LANES
    heads = (width + pad) // DH
    pairs = heads // 2
    if pad:
        keys_all = jnp.pad(keys_all, ((0, 0), (0, 0), (0, pad)))
        values_all = jnp.pad(values_all, ((0, 0), (0, 0), (0, pad)))
        bias_table = jnp.pad(bias_table, ((0, 0), (0, heads - bias_table.shape[1])))
        gain = jnp.pad(gain, (0, heads - gain.shape[0]))
    live = lengths - first_pos
    gain_high, gain_low = split_parts(gain * 0.5, 2)
    gains = jnp.stack([gain_high, gain_low], axis=1).reshape(pairs, 4)
    parts = jnp.stack(split_parts(bias_table * 0.5, 3), axis=0)
    table = jnp.pad(parts.transpose(2, 0, 1), ((0, 0), (0, DH - 3), (0, 0)))
    table = table.reshape(pairs, LANES, bias_table.shape[0]).astype(jnp.bfloat16)
    lane = jnp.arange(LANES, dtype=jnp.int32)[None, None, :]
    hits = cand_ids[:, :, None] == lane % ITEMS
    same = hits.astype(jnp.bfloat16)
    tail = ((hits & (lane < DH)) | ((lane >= DH) & (lane < DH + 3))).astype(jnp.bfloat16)
    return (
        live,
        gains,
        same,
        tail,
        keys_all,
        values_all,
        items[:, None, :],
        buckets[:, None, :],
        table,
    )


def finish(pieces, own_rows, w_gate, w_out, w_up, w_down, norm_gain):
    center = pieces - jnp.mean(pieces, axis=1, keepdims=True)
    normed = (
        center
        * lax.rsqrt(jnp.mean(center * center, axis=1, keepdims=True) + 1e-05)
        * norm_gain[None, :]
    )
    gate_value = silu_value(jnp.dot(own_rows, w_gate, preferred_element_type=jnp.float32))
    mixed = (normed * gate_value).astype(jnp.bfloat16)
    state_sum = own_rows.astype(jnp.float32) + jnp.dot(
        mixed, w_out, preferred_element_type=jnp.float32
    )
    hidden = silu_value(
        jnp.dot(state_sum.astype(jnp.bfloat16), w_up, preferred_element_type=jnp.float32)
    ).astype(jnp.bfloat16)
    return (state_sum + jnp.dot(hidden, w_down, preferred_element_type=jnp.float32)).astype(
        jnp.bfloat16
    )


def local(
    cand_feats,
    w_query,
    w_gate,
    w_out,
    w_up,
    w_down,
    norm_gain,
    cache_keys,
    cache_values,
    history_items,
    buckets,
    lengths,
    cand_ids,
    bucket_bias,
    repeat_bias,
):
    user_count = lengths.shape[0]
    span = cache_keys.shape[1]
    width = cache_keys.shape[2]
    pad = -width % LANES
    packed = pack_tables(
        cache_keys,
        cache_values,
        history_items,
        buckets,
        lengths,
        cand_ids,
        bucket_bias,
        repeat_bias,
        lax.axis_index("seq") * span,
    )
    features = lax.all_gather(cand_feats, "head", axis=1, tiled=True)
    queries_own = jnp.dot(features, w_query, preferred_element_type=jnp.float32).astype(
        jnp.bfloat16
    ) * (0.5 / math.sqrt(DH))
    gathered = lax.all_gather(queries_own, "seq", axis=0, tiled=True)
    if pad:
        gathered = jnp.pad(gathered, ((0, 0), (0, pad)))
    partial_rows = attend(gathered, packed, 0, user_count)[:, :width]
    own_sum = lax.psum_scatter(partial_rows, "seq", scatter_dimension=0, tiled=True)
    pieces = lax.all_to_all(own_sum, "head", split_axis=0, concat_axis=1, tiled=True).astype(
        jnp.float32
    )
    row_count = pieces.shape[0]
    own_rows = lax.dynamic_slice_in_dim(features, lax.axis_index("head") * row_count, row_count, 0)
    return finish(pieces, own_rows, w_gate, w_out, w_up, w_down, norm_gain)


def solution(mesh):
    in_specs = (
        P(("groups", "seq"), "head"),
        P(None, "head"),
        P(),
        P(),
        P(),
        P(),
        P(),
        P("groups", "seq", "head"),
        P("groups", "seq", "head"),
        P("groups", "seq"),
        P("groups", "seq"),
        P("groups"),
        P("groups", None),
        P(None, "head"),
        P("head"),
    )
    out_specs = P(("groups", "seq", "head"), None)
    return jax.shard_map(local, mesh=mesh, in_specs=in_specs, out_specs=out_specs, check_vma=False)
```

time: 767 us -> 398 us (0.52)
  matrix products: 332 us -> 15 us
  Pallas kernels: 0 us -> 147 us
  local copies, waits for them, and re-layouts: 126 us -> 3.28 us
  other arithmetic: 120 us -> 7.11 us
  waiting for transfers between devices: 169 us -> 206 us
    dot_general x34 -> x2, matrix products: 328 us -> 10.5 us  [the longest x1 5.65 us: finish(): jnp.dot(hidden, w_down, preferred_element_type=jnp.float32)]
    pallas_call x0 -> x1, Pallas kernels: none -> 147 us  [attend(): pl.pallas_call(functools.partial(attend_kernel, keys=keys, rows=rows, fir...]
    convert_element_type x32 -> x1, other arithmetic: 107 us -> 5.83 us  [pack_tables(): (hits & (lane < DH) | (lane >= DH) & (lane < DH + 3)).astype(jnp.bfloat16)]
    unnamed x15 -> x19, local copies, waits for them, and re-layouts: 46.8 us -> 0.04 us
    dynamic_slice x48 -> x0, local copies, waits for them, and re-layouts: 37.8 us -> none  [run_users(): lax.map(one_user, (grouped_q, keyed, valued, item_rows, bucket_rows, user...]
    all_gather x1, waiting for transfers between devices: 38.7 us -> 71.1 us  [local(): gathered = lax.all_gather(queries_own, 'seq', axis=0, tiled=True)]
    while x1 -> x0, local copies, waits for them, and re-layouts: 20.2 us -> none  [run_users(): lax.map(one_user, (grouped_q, keyed, valued, item_rows, bucket_rows, user...]
    reshape x1, local copies, waits for them, and re-layouts: 14.7 us -> 0.59 us  [pack_tables(): gains = jnp.stack([gain_high, gain_low], axis=1).reshape(pairs, 4)]
  transfers between devices with their start and end apart: 4 -> 4, of which waited for: 4 -> 4; matrix products, arithmetic and copies ran while one was open for 6% -> 2% of each run, Pallas kernels for 0% -> 0%
where the time goes in v1:
time: 398 us; the launch traced here: 395 us
  waiting for transfers between devices  206 us (52%)
  Pallas kernels  147 us (37%)
  matrix products  15 us (4%)
  between operations  13.2 us (3%)
  other arithmetic  7.11 us (2%)
    pallas_call x1, Pallas kernels, attend(): pl.pallas_call(functools.partial(attend_kernel, keys=keys, rows=rows, fir...  147 us
    reduce_scatter x1, waiting for transfers between devices, local(): lax.psum_scatter(partial_rows, 'seq', scatter_dimension=0, tiled=True)  80.1 us
    all_gather x1, waiting for transfers between devices, local(): gathered = lax.all_gather(queries_own, 'seq', axis=0, tiled=True)  71.1 us
    all_gather x1, waiting for transfers between devices, local(): features = lax.all_gather(cand_feats, 'head', axis=1, tiled=True)  39.3 us
    all_to_all x1, waiting for transfers between devices, local(): lax.all_to_all(own_sum, 'head', split_axis=0, concat_axis=1, tiled=True)  14.4 us
  transfers between devices with their start and end apart: 4, of which 4 were waited for; matrix products, arithmetic and copies ran while one was open for 2% of the time, Pallas kernels for 0%

profile of v1, /device:TPU:0, one launch (start us, length us, event | category | flops | bytes accessed | tf_op | source)
XLA Modules:
  0.0 395.2 jit_solution(15352210316957599149)
XLA Ops:
  6.5 0.7 all-gather.3.cloned.1.call-update
  7.3 0.0 all-gather.5.cloned.1.call-start
  7.3 39.3 %all-gather.3.cloned.1.call-done = bf16[4096,512]{1,0:T(8,128)(2,1)} async-done(((bf16[4096,128]{1,0:T(8,128)(2,1)}), bf16[4096,512]{1,0:T(8,128)(2,1)}) %all-gather.3.cloned.1.call-update) | async-done | bytes 4194320 | tf_op jit(solution)/shard_map/all_gather | solution.py:239
  46.6 4.4 %fusion.2 = bf16[4096,128]{1,0:T(8,128)(2,1)} fusion(bf16[4096,512]{1,0:T(8,128)(2,1)} %all-gather.3.cloned.1.call-done, bf16[512,128]{1,0:T(8,128)(2,1)} %param.16), kind=kOutput, calls=%fused_computation.5 | convolution fusion | flops 537919488 | bytes 5373952 | tf_op jit(solution)/shard_map/dot_general | solution.py:240
  51.1 0.0 all-gather.5.cloned.1.call-update
  51.1 0.0 reduce-scatter.2.cloned.1.call-start
  51.2 0.1 copy.16
  51.3 0.6 reshape.72.gain_ref
  51.9 1.0 broadcast_in_dim.4.item_ref
  52.9 1.0 broadcast_in_dim.5.bucket_ref
  53.9 0.6 pad.5.clone
  54.5 0.5 broadcast_subtract_fusion.live_ref
  55.0 5.8 %fusion.1 = (bf16[16,1024,128]{2,1,0:T(8,128)(2,1)}, bf16[16,1024,128]{2,1,0:T(8,128)(2,1)}) fusion(s32[128]{0:T(128)S(1)} %and_select_fusion, s32[16,1024]{1,0:T(8,128)S(1)} %copy-done.3, pred[128]{0:T(512)(128)(4,1)S(1)} %get-tuple-element.12, pred[128]{0:T(512)(128)(4,1)S(1)} %get-tuple-element.13), kind=kLoop, calls=%fused_computation.3 | loop fusion | flops 10485760 | bytes 8454912 | tf_op jit(solution)/shard_map/convert_element_type | solution.py:173
  60.8 71.1 %all-gather.5.cloned.1.call-done.q_ref = bf16[16384,128]{1,0:T(8,128)(2,1)} async-done(((bf16[4096,128]{1,0:T(8,128)(2,1)}), bf16[16384,128]{1,0:T(8,128)(2,1)}) %all-gather.5.cloned.1.call-update) | async-done | bytes 4194320 | tf_op jit(solution)/shard_map/all_gather | solution.py:243
  132.0 147.2 %shard_map.145 = bf16[16384,128]{1,0:T(8,128)(2,1)} custom-call(s32[16]{0:T(128)} %broadcast_subtract_fusion.live_ref, f32[1,4]{1,0:T(1,128)} %reshape.72.gain_ref, bf16[16384,128]{1,0:T(8,128)(2,1)} %all-gather.5.cloned.1.call-done.q_ref, bf16[16,1024,128]{2,1,0:T(8,128)(2,1)} %get-tuple-element.6.same_ref, ...), custom_call_target="tpu_custom_call" | custom-call | flops 68719476736 | bytes 41943040 | tf_op jit(solution)/shard_map/pallas_call | solution.py:111
  279.2 0.0 reduce-scatter.2.cloned.1.call-update
  279.2 80.1 %reduce-scatter.2.cloned.1.call-done = bf16[4096,128]{1,0:T(8,128)(2,1)} async-done(((bf16[16384,128]{1,0:T(8,128)(2,1)}), bf16[4096,128]{1,0:T(8,128)(2,1)}) %reduce-scatter.2.cloned.1.call-update) | async-done | bytes 1048592 | tf_op jit(solution)/shard_map/reduce_scatter | solution.py:247
  359.4 3.6 all-to-all-start
  363.0 14.4 %all-to-all-done = bf16[4,1024,128]{2,1,0:T(8,128)(2,1)S(1)} async-done(((bf16[4,1024,128]{2,1,0:T(8,128)(2,1)}), bf16[4,1024,128]{2,1,0:T(8,128)(2,1)S(1)}, u32[]{:S(2)}, u32[]{:S(2)}) %all-to-all-start) | async-done | bytes 1048608 | tf_op jit(solution)/shard_map/all_to_all | solution.py:248
  377.4 0.2 convert_reduce_fusion
  377.6 0.5 fusion.4
  378.2 0.0 copy-start.5
  378.2 4.9 %convert_add_fusion = f32[1024,512]{1,0:T(8,128)} fusion(bf16[512,512]{1,0:T(8,128)(2,1)} %param.18, f32[512]{0:T(512)S(1)} %copy-done.6, f32[1024]{0:T(1024)S(1)} %add_rsqrt_fusion, f32[1024]{0:T(1024)S(1)} %broadcast_multiply_fusion, bf16[4096,512]{1,0:T(8,128)(2,1)} %all-gather.3.cloned.1.call-done, s32[]{:T(128)S(6)} %select_n.15, ...), kind=kOutput, calls=%fused_computation.18 | convolution fusion | flops 1079508992 | bytes 6302720 | tf_op jit(solution)/shard_map/dot_general | solution.py:196
  383.1 5.7 %add_convert_fusion = bf16[1024,512]{1,0:T(8,128)(2,1)} fusion(f32[1024,512]{1,0:T(8,128)} %convert_add_fusion, bf16[1024,512]{1,0:T(8,128)(2,1)S(1)} %copy-done, bf16[512,1024]{1,0:T(8,128)(2,1)S(1)} %copy-done.5), kind=kOutput, calls=%fused_computation.17 | convolution fusion | flops 2153250816 | bytes 5242880 | tf_op jit(solution)/shard_map/dot_general | solution.py:202
  (27 shorter events, 0.1 us)
Async XLA Ops:
  6.5 376.5 %copy-start = (bf16[1024,512]{1,0:T(8,128)(2,1)S(1)}, bf16[1024,512]{1,0:T(8,128)(2,1)}, u32[]{:S(2)}) copy-start(bf16[1024,512]{1,0:T(8,128)(2,1)} %param.20) | copy-start | bytes 3145732
  6.5 40.1 %all-gather.3.cloned.1.call-start = ((), (), s32[]{:S(2)}) async-start(), calls=%async_computation.2 | async-start | bytes 5242880 | tf_op jit(solution)/shard_map/all_gather | solution.py:239
  7.3 43.9 %copy-start.7 = (f32[2]{0:T(128)S(1)}, f32[2]{0:T(128)}, u32[]{:S(2)}) copy-start(f32[2]{0:T(128)} %param.29) | copy-start | bytes 28
  7.3 44.6 %copy-start.4 = (f32[128,2]{0,1:T(2,128)S(1)}, f32[128,2]{0,1:T(2,128)}, u32[]{:S(2)}) copy-start(f32[128,2]{0,1:T(2,128)} %param.28) | copy-start | bytes 3076
  7.3 44.6 %copy-start.1 = (s32[16,4096]{1,0:T(8,128)S(1)}, s32[16,4096]{1,0:T(8,128)}, u32[]{:S(2)}) copy-start(s32[16,4096]{1,0:T(8,128)} %param.24) | copy-start | bytes 786436
  7.3 45.6 %copy-start.2 = (s32[16,4096]{1,0:T(8,128)S(1)}, s32[16,4096]{1,0:T(8,128)}, u32[]{:S(2)}) copy-start(s32[16,4096]{1,0:T(8,128)} %param.25) | copy-start | bytes 786436
  7.3 124.7 %all-gather.5.cloned.1.call-start = ((), (), s32[]{:S(2)}) async-start(), calls=%async_computation.3 | async-start | bytes 5242880 | tf_op jit(solution)/shard_map/all_gather | solution.py:243
  51.0 3.4 copy-start.8
  51.1 3.9 copy-start.3
  51.1 308.3 %reduce-scatter.2.cloned.1.call-start = ((), (), s32[]{:S(2)}) async-start(), calls=%async_computation.4 | async-start | bytes 5242880 | tf_op jit(solution)/shard_map/reduce_scatter | solution.py:247
  359.4 18.8 %copy-start.6 = (f32[512]{0:T(512)S(1)}, f32[512]{0:T(512)}, u32[]{:S(2)}) copy-start(f32[512]{0:T(512)} %param.21) | copy-start | bytes 6148
  359.4 18.1 %all-to-all-start = ((bf16[4,1024,128]{2,1,0:T(8,128)(2,1)}), bf16[4,1024,128]{2,1,0:T(8,128)(2,1)S(1)}, u32[]{:S(2)}, u32[]{:S(2)}) async-start(bf16[4,1024,128]{2,1,0:T(8,128)(2,1)} %bitcast.36), calls=%async_computation.1 | async-start | bytes 2097152 | tf_op jit(solution)/shard_map/all_to_all | solution.py:248
  378.2 4.9 %copy-start.5 = (bf16[512,1024]{1,0:T(8,128)(2,1)S(1)}, bf16[512,1024]{1,0:T(8,128)(2,1)}, u32[]{:S(2)}) copy-start(bf16[512,1024]{1,0:T(8,128)(2,1)} %param.19) | copy-start | bytes 3145732
Sparse Core Ops, SparseCore 0:
  8.9 37.7 all-gather.2
  51.2 80.7 all-gather.4
  279.3 79.9 reduce-scatter.1

commit v2 on v1

--- a/solution.py
+++ b/solution.py
@@ -37,11 +37,12 @@
     *,
     keys,
     rows,
-    first_user,
+    offset,
+    stride,
 ):
     pair = pl.program_id(0)
     user = pl.program_id(1)
-    live = live_ref[first_user + user]
+    live = live_ref[user * stride + offset]
     low_lanes = lax.broadcasted_iota(jnp.int32, (1, LANES), 1) < DH
     low_row = low_lanes.astype(jnp.bfloat16)
     high_row = 1 - low_row
@@ -97,25 +98,27 @@
     out_ref[...] = total[...].astype(out_ref.dtype)
 
 
-def attend(queries, packed, first_user, user_count):
+def attend(queries, packed, offset, stride, base=0, user_count=None):
     live, gains, same, tail, keys_all, values_all, items, buckets, table = packed
     per_user = same.shape[1]
+    user_count = user_count or queries.shape[0] // per_user
+    offset = offset + base * stride
     width = queries.shape[1]
     pairs = width // LANES
     span = keys_all.shape[1]
     keys = math.gcd(span, KEYS)
     rows = math.gcd(per_user, ROWS)
-    of_user = lambda p, u, *_: (first_user + u, 0, 0)
-    of_pair = lambda p, u, *_: (first_user + u, 0, p)
+    of_user = lambda p, u, *_: (u * stride + offset, 0, 0)
+    of_pair = lambda p, u, *_: (u * stride + offset, 0, p)
     scores = user_count * per_user * span * 2 * pairs
     return pl.pallas_call(
-        functools.partial(attend_kernel, keys=keys, rows=rows, first_user=first_user),
-        out_shape=jax.ShapeDtypeStruct(queries.shape, jnp.bfloat16),
+        functools.partial(attend_kernel, keys=keys, rows=rows, offset=offset, stride=stride),
+        out_shape=jax.ShapeDtypeStruct((user_count * per_user, width), jnp.bfloat16),
         grid_spec=pltpu.PrefetchScalarGridSpec(
             num_scalar_prefetch=2,
             grid=(pairs, user_count),
             in_specs=[
-                pl.BlockSpec((per_user, LANES), lambda p, u, *_: (u, p)),
+                pl.BlockSpec((per_user, LANES), lambda p, u, *_: (u + base, p)),
                 pl.BlockSpec((1, per_user, LANES), of_user),
                 pl.BlockSpec((1, per_user, LANES), of_user),
                 pl.BlockSpec((1, span, LANES), of_pair),
@@ -221,7 +224,6 @@
     bucket_bias,
     repeat_bias,
 ):
-    user_count = lengths.shape[0]
     span = cache_keys.shape[1]
     width = cache_keys.shape[2]
     pad = -width % LANES
@@ -236,20 +238,73 @@
         repeat_bias,
         lax.axis_index("seq") * span,
     )
-    features = lax.all_gather(cand_feats, "head", axis=1, tiled=True)
-    queries_own = jnp.dot(features, w_query, preferred_element_type=jnp.float32).astype(
-        jnp.bfloat16
-    ) * (0.5 / math.sqrt(DH))
-    gathered = lax.all_gather(queries_own, "seq", axis=0, tiled=True)
-    if pad:
-        gathered = jnp.pad(gathered, ((0, 0), (0, pad)))
-    partial_rows = attend(gathered, packed, 0, user_count)[:, :width]
-    own_sum = lax.psum_scatter(partial_rows, "seq", scatter_dimension=0, tiled=True)
+    heads = lax.axis_size("head")
+    per_user = cand_ids.shape[1]
+    own_users = cand_feats.shape[0] // per_user
+
+    def project(features):
+        product = jnp.dot(features, w_query, preferred_element_type=jnp.float32)
+        return product.astype(jnp.bfloat16) * (0.5 / math.sqrt(DH))
+
+    if cand_feats.shape[0] % per_user or own_users != heads:
+        features = lax.all_gather(cand_feats, "head", axis=1, tiled=True)
+        gathered = lax.all_gather(project(features), "seq", axis=0, tiled=True)
+        if pad:
+            gathered = jnp.pad(gathered, ((0, 0), (0, pad)))
+        partial_rows = attend(gathered, packed, 0, 1)[:, :width]
+        own_sum = lax.psum_scatter(partial_rows, "seq", scatter_dimension=0, tiled=True)
+        row_count = cand_feats.shape[0] // heads
+        own_rows = lax.dynamic_slice_in_dim(
+            features, lax.axis_index("head") * row_count, row_count, 0
+        )
+    else:
+        shards = lax.axis_size("seq")
+        after = lax.optimization_barrier
+        rows = [cand_feats[user * per_user : (user + 1) * per_user] for user in range(own_users)]
+
+        def over_head(user):
+            return lax.all_gather(rows[user], "head", axis=1, tiled=True)
+
+        def over_seq(queries):
+            whole = lax.all_gather(queries, "seq", axis=0, tiled=True)
+            return jnp.pad(whole, ((0, 0), (0, pad))) if pad else whole
+
+        def summed(part):
+            return lax.psum_scatter(part[:, :width], "seq", scatter_dimension=0, tiled=True)
+
+        features = [over_head(0)]
+        arrived = [over_seq(project(features[0]))]
+        for user in range(1, min(3, own_users)):
+            rows[user], arrived[0] = after((rows[user], arrived[0]))
+            features.append(over_head(user))
+        early = max(1, shards // 2)
+        part = attend(arrived[0], packed, 0, own_users, 0, early)
+        sums = []
+        for user in range(own_users):
+            if user + 1 < own_users:
+                features[user + 1], part = after((features[user + 1], part))
+                queries = project(features[user + 1])
+                queries, arrived[user] = after((queries, arrived[user]))
+                arrived.append(over_seq(queries))
+            if user == 0:
+                if shards > early:
+                    rest = attend(arrived[0], packed, 0, own_users, early, shards - early)
+                    part = jnp.concatenate([part, rest], axis=0)
+            else:
+                arrived[user], part = after((arrived[user], part))
+                sums.append(summed(part))
+                part = attend(arrived[user], packed, user, own_users)
+            if user + 3 < own_users:
+                rows[user + 3], part = after((rows[user + 3], part))
+                features.append(over_head(user + 3))
+        sums.append(summed(part))
+        own_rows = features[0]
+        for user in range(1, own_users):
+            own_rows = jnp.where(lax.axis_index("head") == user, features[user], own_rows)
+        own_sum = jnp.concatenate(sums, axis=0)
     pieces = lax.all_to_all(own_sum, "head", split_axis=0, concat_axis=1, tiled=True).astype(
         jnp.float32
     )
-    row_count = pieces.shape[0]
-    own_rows = lax.dynamic_slice_in_dim(features, lax.axis_index("head") * row_count, row_count, 0)
     return finish(pieces, own_rows, w_gate, w_out, w_up, w_down, norm_gain)
 
 

time: 398 us -> 354 us (0.89)
  waiting for transfers between devices: 206 us -> 144 us
  Pallas kernels: 147 us -> 153 us
  matrix products: 15 us -> 20.8 us
  other arithmetic: 7.11 us -> 11.4 us
    all_gather x2 -> x8, waiting for transfers between devices: 110 us -> 70.2 us  [the longest x4 50.5 us: over_seq(): whole = lax.all_gather(queries, 'seq', axis=0, tiled=True)]
    reduce_scatter x1 -> x4, waiting for transfers between devices: 80.1 us -> 57.8 us  [summed(): lax.psum_scatter(part[:, :width], 'seq', scatter_dimension=0, tiled=True)]
    pallas_call x1 -> x5, Pallas kernels: 147 us -> 153 us  [attend(): pl.pallas_call(functools.partial(attend_kernel, keys=keys, rows=rows, off...]
    dot_general x1 -> x4, matrix products: 4.41 us -> 9.49 us  [project(): product = jnp.dot(features, w_query, preferred_element_type=jnp.float32)]
    concatenate x0 -> x2, other arithmetic: none -> 4.33 us  [the longest x1 2.22 us: local(): own_sum = jnp.concatenate(sums, axis=0)]
  transfers between devices with their start and end apart: 4 -> 13, of which waited for: 4 -> 8; matrix products, arithmetic and copies ran while one was open for 2% -> 5% of each run, Pallas kernels for 0% -> 43%
where the time goes in v2:
time: 354 us; the launch traced here: 353 us
  Pallas kernels  153 us (43%)
  waiting for transfers between devices  144 us (41%)
  matrix products  20.8 us (6%)
  between operations  13.7 us (4%)
  other arithmetic  11.4 us (3%)
  local copies, waits for them, and re-layouts  5.55 us (2%)
  starting transfers between devices  4.31 us (1%)
    pallas_call x5, Pallas kernels, attend(): pl.pallas_call(functools.partial(attend_kernel, keys=keys, rows=rows, off...  153 us
    reduce_scatter x4, waiting for transfers between devices, summed(): lax.psum_scatter(part[:, :width], 'seq', scatter_dimension=0, tiled=True)  57.8 us
    all_gather x4, waiting for transfers between devices, over_seq(): whole = lax.all_gather(queries, 'seq', axis=0, tiled=True)  50.5 us
    all_gather x4, waiting for transfers between devices, over_head(): return lax.all_gather(rows[user], 'head', axis=1, tiled=True)  19.7 us
    all_to_all x1, waiting for transfers between devices, local(): lax.all_to_all(own_sum, 'head', split_axis=0, concat_axis=1, tiled=True)  14.4 us
    dot_general x4, matrix products, project(): product = jnp.dot(features, w_query, preferred_element_type=jnp.float32)  9.49 us
  transfers between devices with their start and end apart: 13, of which 8 were waited for; matrix products, arithmetic and copies ran while one was open for 5% of the time, Pallas kernels for 43%

profile of v2, /device:TPU:0, one launch (start us, length us, event | category | flops | bytes accessed | tf_op | source)
XLA Modules:
  0.0 353.1 jit_solution(6958909418267305149)
XLA Ops:
  6.6 2.3 fusion.30
  9.0 19.6 %all-gather.9.cloned.1.call-done = bf16[1024,512]{1,0:T(8,128)(2,1)} async-done(((bf16[1024,128]{1,0:T(8,128)(2,1)}), bf16[1024,512]{1,0:T(8,128)(2,1)}) %all-gather.9.cloned.1.call-update) | async-done | bytes 1048592 | tf_op jit(solution)/shard_map/all_gather | solution.py:266
  28.6 2.4 fusion.11
  31.1 28.1 %all-gather.11.cloned.1.call-done.q_ref = bf16[4096,128]{1,0:T(8,128)(2,1)} async-done(((bf16[1024,128]{1,0:T(8,128)(2,1)}), bf16[4096,128]{1,0:T(8,128)(2,1)}) %all-gather.11.cloned.1.call-update) | async-done | bytes 1048592 | tf_op jit(solution)/shard_map/all_gather | solution.py:269
  63.2 5.7 %fusion.1 = (bf16[16,1024,128]{2,1,0:T(8,128)(2,1)}, bf16[16,1024,128]{2,1,0:T(8,128)(2,1)}) fusion(s32[128]{0:T(128)S(1)} %and_select_fusion, s32[16,1024]{1,0:T(8,128)S(1)} %copy-done.6, pred[128]{0:T(512)(128)(4,1)S(1)} %get-tuple-element.64, pred[128]{0:T(512)(128)(4,1)S(1)} %get-tuple-element.65), kind=kLoop, calls=%fused_computation.3 | loop fusion | flops 10485760 | bytes 8454912 | tf_op jit(solution)/shard_map/convert_element_type | solution.py:176
  69.0 16.7 %shard_map.145 = bf16[2048,128]{1,0:T(8,128)(2,1)} custom-call(s32[16]{0:T(128)} %broadcast_subtract_fusion.live_ref, f32[1,4]{1,0:T(1,128)} %reshape.72.gain_ref, bf16[4096,128]{1,0:T(8,128)(2,1)} %all-gather.11.cloned.1.call-done.q_ref, bf16[16,1024,128]{2,1,0:T(8,128)(2,1)} %get-tuple-element.58.same_ref, ...), custom_call_target="tpu_custom_call" | custom-call | flops 8589934592 | bytes 5242880 | tf_op jit(solution)/shard_map/pallas_call | solution.py:114
  85.7 2.4 fusion.12
  88.1 16.8 %shard_map.146 = bf16[2048,128]{1,0:T(8,128)(2,1)} custom-call(s32[16]{0:T(128)} %broadcast_subtract_fusion.live_ref, f32[1,4]{1,0:T(1,128)} %reshape.72.gain_ref, bf16[4096,128]{1,0:T(8,128)(2,1)} %all-gather.11.cloned.1.call-done.q_ref, bf16[16,1024,128]{2,1,0:T(8,128)(2,1)} %get-tuple-element.58.same_ref, ...), custom_call_target="tpu_custom_call" | custom-call | flops 8589934592 | bytes 5242880 | tf_op jit(solution)/shard_map/pallas_call | solution.py:114
  104.9 2.1 pad_maximum_fusion
  107.1 2.4 fusion.13
  109.5 15.1 %all-gather.19.cloned.1.call-done.q_ref = bf16[4096,128]{1,0:T(8,128)(2,1)} async-done(((bf16[1024,128]{1,0:T(8,128)(2,1)}), bf16[4096,128]{1,0:T(8,128)(2,1)}) %all-gather.19.cloned.1.call-update) | async-done | bytes 1048592 | tf_op jit(solution)/shard_map/all_gather | solution.py:269
  124.7 37.5 %shard_map.147 = bf16[4096,128]{1,0:T(8,128)(2,1)} custom-call(s32[16]{0:T(128)} %broadcast_subtract_fusion.live_ref, f32[1,4]{1,0:T(1,128)} %reshape.72.gain_ref, bf16[4096,128]{1,0:T(8,128)(2,1)} %all-gather.19.cloned.1.call-done.q_ref, bf16[16,1024,128]{2,1,0:T(8,128)(2,1)} %get-tuple-element.58.same_ref, ...), custom_call_target="tpu_custom_call" | custom-call | flops 17179869184 | bytes 10485760 | tf_op jit(solution)/shard_map/pallas_call | solution.py:114
  162.2 2.4 fusion.14
  164.5 7.3 %all-gather.21.cloned.1.call-done.q_ref = bf16[4096,128]{1,0:T(8,128)(2,1)} async-done(((bf16[1024,128]{1,0:T(8,128)(2,1)}), bf16[4096,128]{1,0:T(8,128)(2,1)}) %all-gather.21.cloned.1.call-update) | async-done | bytes 1048592 | tf_op jit(solution)/shard_map/all_gather | solution.py:269
  173.4 45.0 %shard_map.148 = bf16[4096,128]{1,0:T(8,128)(2,1)} custom-call(s32[16]{0:T(128)} %broadcast_subtract_fusion.live_ref, f32[1,4]{1,0:T(1,128)} %reshape.72.gain_ref, bf16[4096,128]{1,0:T(8,128)(2,1)} %all-gather.21.cloned.1.call-done.q_ref, bf16[16,1024,128]{2,1,0:T(8,128)(2,1)} %get-tuple-element.58.same_ref, ...), custom_call_target="tpu_custom_call" | custom-call | flops 17179869184 | bytes 10485760 | tf_op jit(solution)/shard_map/pallas_call | solution.py:114
  218.5 37.5 %shard_map.149 = bf16[4096,128]{1,0:T(8,128)(2,1)} custom-call(s32[16]{0:T(128)} %broadcast_subtract_fusion.live_ref, f32[1,4]{1,0:T(1,128)} %reshape.72.gain_ref, bf16[4096,128]{1,0:T(8,128)(2,1)} %all-gather.23.cloned.1.call-done.q_ref, bf16[16,1024,128]{2,1,0:T(8,128)(2,1)} %get-tuple-element.58.same_ref, ...), custom_call_target="tpu_custom_call" | custom-call | flops 17179869184 | bytes 10485760 | tf_op jit(solution)/shard_map/pallas_call | solution.py:114
  256.1 1.7 reduce-scatter.7.cloned.1.call-done
  257.8 28.1 %reduce-scatter.9.cloned.1.call-done = bf16[1024,128]{1,0:T(8,128)(2,1)} async-done(((bf16[4096,128]{1,0:T(8,128)(2,1)}), bf16[1024,128]{1,0:T(8,128)(2,1)}) %reduce-scatter.9.cloned.1.call-update) | async-done | bytes 262160 | tf_op jit(solution)/shard_map/reduce_scatter | solution.py:273
  285.9 28.0 %reduce-scatter.11.cloned.1.call-done = bf16[1024,128]{1,0:T(8,128)(2,1)} async-done(((bf16[4096,128]{1,0:T(8,128)(2,1)}), bf16[1024,128]{1,0:T(8,128)(2,1)}) %reduce-scatter.11.cloned.1.call-update) | async-done | bytes 262160 | tf_op jit(solution)/shard_map/reduce_scatter | solution.py:273
  313.9 2.2 pad_maximum_fusion.1
  316.1 3.6 %all-to-all-start = ((bf16[4,1024,128]{2,1,0:T(8,128)(2,1)}), bf16[4,1024,128]{2,1,0:T(8,128)(2,1)S(1)}, u32[]{:S(2)}, u32[]{:S(2)}) async-start(bf16[4,1024,128]{2,1,0:T(8,128)(2,1)} %bitcast.7), calls=%async_computation.4 | async-start | bytes 2097152 | tf_op jit(solution)/shard_map/all_to_all | solution.py:305
  319.8 14.4 %all-to-all-done = bf16[4,1024,128]{2,1,0:T(8,128)(2,1)S(1)} async-done(((bf16[4,1024,128]{2,1,0:T(8,128)(2,1)}), bf16[4,1024,128]{2,1,0:T(8,128)(2,1)S(1)}, u32[]{:S(2)}, u32[]{:S(2)}) %all-to-all-start) | async-done | bytes 1048608 | tf_op jit(solution)/shard_map/all_to_all | solution.py:305
  334.9 5.4 %convert_add_fusion = f32[1024,512]{1,0:T(8,128)} fusion(bf16[512,512]{1,0:T(8,128)(2,1)} %param.18, f32[512]{0:T(512)S(1)} %copy-done.8, f32[1024]{0:T(1024)S(1)} %add_rsqrt_fusion, f32[1024]{0:T(1024)S(1)} %broadcast_multiply_fusion, bf16[512,512]{1,0:T(8,128)(2,1)} %param.17, bf16[1024,512]{1,0:T(8,128)(2,1)} %all-gather.15.cloned.1.call-done, ...), kind=kOutput, calls=%fused_computation.16 | convolution fusion | flops 1082654720 | bytes 8398851 | tf_op jit(solution)/shard_map/dot_general | solution.py:199
  340.3 6.0 %add_convert_fusion = bf16[1024,512]{1,0:T(8,128)(2,1)} fusion(f32[1024,512]{1,0:T(8,128)} %convert_add_fusion, bf16[1024,512]{1,0:T(8,128)(2,1)S(1)} %copy-done, bf16[512,1024]{1,0:T(8,128)(2,1)} %param.19), kind=kOutput, calls=%fused_computation.15 | convolution fusion | flops 2153250816 | bytes 5242880 | tf_op jit(solution)/shard_map/dot_general | solution.py:205
  (68 shorter events, 6.7 us)
Async XLA Ops:
  6.5 333.8 %copy-start = (bf16[1024,512]{1,0:T(8,128)(2,1)S(1)}, bf16[1024,512]{1,0:T(8,128)(2,1)}, u32[]{:S(2)}) copy-start(bf16[1024,512]{1,0:T(8,128)(2,1)} %param.20) | copy-start | bytes 3145732
  6.5 22.1 %copy-start.2 = (bf16[512,128]{1,0:T(8,128)(2,1)S(1)}, bf16[512,128]{1,0:T(8,128)(2,1)}, u32[]{:S(2)}) copy-start(bf16[512,128]{1,0:T(8,128)(2,1)} %param.16) | copy-start | bytes 393220
  6.5 52.7 %copy-start.9 = (f32[2]{0:T(128)S(1)}, f32[2]{0:T(128)}, u32[]{:S(2)}) copy-start(f32[2]{0:T(128)} %param.29) | copy-start | bytes 28
  6.5 53.4 %copy-start.7 = (f32[128,2]{0,1:T(2,128)S(1)}, f32[128,2]{0,1:T(2,128)}, u32[]{:S(2)}) copy-start(f32[128,2]{0,1:T(2,128)} %param.28) | copy-start | bytes 3076
  6.5 53.4 %copy-start.4 = (s32[16,4096]{1,0:T(8,128)S(1)}, s32[16,4096]{1,0:T(8,128)}, u32[]{:S(2)}) copy-start(s32[16,4096]{1,0:T(8,128)} %param.24) | copy-start | bytes 786436
  6.5 54.4 %copy-start.5 = (s32[16,4096]{1,0:T(8,128)S(1)}, s32[16,4096]{1,0:T(8,128)}, u32[]{:S(2)}) copy-start(s32[16,4096]{1,0:T(8,128)} %param.25) | copy-start | bytes 786436
  6.6 22.1 %all-gather.9.cloned.1.call-start = ((), (), s32[]{:S(2)}) async-start(), calls=%async_computation.5 | async-start | bytes 1310720 | tf_op jit(solution)/shard_map/all_gather | solution.py:266
  8.9 53.7 %copy-start.10 = (s32[16]{0:T(128)S(1)}, s32[16]{0:T(128)}, u32[]{:S(2)}) copy-start(s32[16]{0:T(128)} %param.26) | copy-start | bytes 196
  8.9 54.3 %copy-start.6 = (s32[16,1024]{1,0:T(8,128)S(1)}, s32[16,1024]{1,0:T(8,128)}, u32[]{:S(2)}) copy-start(s32[16,1024]{1,0:T(8,128)} %param.27) | copy-start | bytes 196612
  8.9 50.2 %all-gather.11.cloned.1.call-start = ((), (), s32[]{:S(2)}) async-start(), calls=%async_computation.6 | async-start | bytes 1310720 | tf_op jit(solution)/shard_map/all_gather | solution.py:269
  31.0 54.6 %all-gather.13.cloned.1.call-start = ((), (), s32[]{:S(2)}) async-start(), calls=%async_computation.7 | async-start | bytes 1310720 | tf_op jit(solution)/shard_map/all_gather | solution.py:266
  59.2 47.9 %all-gather.17.cloned.1.call-start = ((), (), s32[]{:S(2)}) async-start(), calls=%async_computation.9 | async-start | bytes 1310720 | tf_op jit(solution)/shard_map/all_gather | solution.py:266
  63.2 61.5 %all-gather.19.cloned.1.call-start = ((), (), s32[]{:S(2)}) async-start(), calls=%async_computation.10 | async-start | bytes 1310720 | tf_op jit(solution)/shard_map/all_gather | solution.py:269
  88.1 16.9 %copy-start.1 = (bf16[2048,128]{1,0:T(8,128)(2,1)S(1)}, bf16[2048,128]{1,0:T(8,128)(2,1)}, u32[]{:S(2)}) copy-start(bf16[2048,128]{1,0:T(8,128)(2,1)} %shard_map.145) | copy-start | bytes 1572868
  88.1 74.1 %all-gather.15.cloned.1.call-start = ((), (), s32[]{:S(2)}) async-start(), calls=%async_computation.8 | async-start | bytes 1310720 | tf_op jit(solution)/shard_map/all_gather | solution.py:266
  107.0 64.8 %all-gather.21.cloned.1.call-start = ((), (), s32[]{:S(2)}) async-start(), calls=%async_computation.12 | async-start | bytes 1310720 | tf_op jit(solution)/shard_map/all_gather | solution.py:269
  124.7 93.8 %all-gather.23.cloned.1.call-start = ((), (), s32[]{:S(2)}) async-start(), calls=%async_computation.14 | async-start | bytes 1310720 | tf_op jit(solution)/shard_map/all_gather | solution.py:269
  171.9 84.2 %reduce-scatter.5.cloned.1.call-start = ((), (), s32[]{:S(2)}) async-start(), calls=%async_computation.11 | async-start | bytes 1310720 | tf_op jit(solution)/shard_map/reduce_scatter | solution.py:273
  172.6 85.2 %reduce-scatter.7.cloned.1.call-start = ((), (), s32[]{:S(2)}) async-start(), calls=%async_computation.13 | async-start | bytes 1310720 | tf_op jit(solution)/shard_map/reduce_scatter | solution.py:273
  173.2 112.7 %reduce-scatter.9.cloned.1.call-start = ((), (), s32[]{:S(2)}) async-start(), calls=%async_computation.15 | async-start | bytes 1310720 | tf_op jit(solution)/shard_map/reduce_scatter | solution.py:273
  218.5 95.4 %reduce-scatter.11.cloned.1.call-start = ((), (), s32[]{:S(2)}) async-start(), calls=%async_computation.16 | async-start | bytes 1310720 | tf_op jit(solution)/shard_map/reduce_scatter | solution.py:273
  316.1 18.8 %copy-start.3 = (bf16[1024,512]{1,0:T(8,128)(2,1)S(1)}, bf16[1024,512]{1,0:T(8,128)(2,1)}, u32[]{:S(2)}) copy-start(bf16[1024,512]{1,0:T(8,128)(2,1)} %all-gather.9.cloned.1.call-done) | copy-start | bytes 3145732
  316.1 18.8 %copy-start.8 = (f32[512]{0:T(512)S(1)}, f32[512]{0:T(512)}, u32[]{:S(2)}) copy-start(f32[512]{0:T(512)} %param.21) | copy-start | bytes 6148
  316.1 18.1 %all-to-all-start = ((bf16[4,1024,128]{2,1,0:T(8,128)(2,1)}), bf16[4,1024,128]{2,1,0:T(8,128)(2,1)S(1)}, u32[]{:S(2)}, u32[]{:S(2)}) async-start(bf16[4,1024,128]{2,1,0:T(8,128)(2,1)} %bitcast.7), calls=%async_computation.4 | async-start | bytes 2097152 | tf_op jit(solution)/shard_map/all_to_all | solution.py:305
Sparse Core Ops, SparseCore 0:
  9.0 19.5 all-gather.8
  31.1 27.9 all-gather.10
  60.7 16.1 all-gather.12
  78.3 16.8 all-gather.16
  96.6 27.9 all-gather.18
  126.0 16.1 all-gather.14
  143.8 27.9 all-gather.20
  173.4 27.3 all-gather.22
  203.1 26.6 reduce-scatter.4
  232.0 25.7 reduce-scatter.6
  260.1 25.7 reduce-scatter.8
  288.0 25.7 reduce-scatter.10
